TPU v7x, 256 devices: a whole 4x4x8 slice. The times are simulated.
256 devices in a mesh: rows: 16 (over z, core), samp: 16 (over y, x).
Axes of the slice: x: 4, y: 4, z: 8, core: 2. Of those that a mesh axis runs over, the one named last changes fastest.
Arguments:
- right_sides: float32 [576, 128, 2048], P('rows', None, 'samp'), may hold values from -6 to 6
- factor_blocks: float32 [576, 6, 128, 128], P('rows', None, 'samp'), may hold values from -0.21875 to 0.21875
- block_columns: int32 [576, 6], P('rows'), may hold values from 0 to 8, as said below
- pivot_rows: int32 [8], replicated, may hold values from 0 to 575, as said below
- diag_inverse: float32 [8, 128, 128], replicated
Outputs:
- solved_blocks: float32 [8, 128, 2048], P(None, None, 'samp')
- updated_sides: float32 [576, 128, 2048], P('rows', None, 'samp')
Inputs may be any that keep to these rules, and one draw needn't show every extreme that they name: `block_columns`: in each block row the values below 8 are distinct; 8 marks an empty slot. `pivot_rows`: the 8 positions are distinct.
All inputs are finite; a program needn't handle non-finite values.
Results may differ from a plain program's by a relative error of at most 0.0001.
Values sent between devices are 32-bit elements; how exact they have to be, the bound alone decides.
No kernel may reach another device: no remote copies, remote signals or barrier semaphores. Data moves between devices by JAX's collectives and lax.ppermute only.
A program may use at most 128 MiB of HBM per device.

v0:
```python
import jax
import jax.numpy as jnp
from jax import lax
from jax.sharding import PartitionSpec as P


def spread(block, axis, source):
    block = jnp.where(lax.axis_index(axis) == source, block, jnp.zeros_like(block))
    return lax.psum(block, axis)


def local(right_sides, factor_blocks, block_columns, pivot_rows, diag_inverse):
    highest = lax.Precision.HIGHEST
    row_count = right_sides.shape[0]
    step_count = pivot_rows.shape[0]
    local_ids = lax.axis_index("rows") * row_count + jnp.arange(row_count, dtype=jnp.int32)
    matches = local_ids[:, None] == pivot_rows[None, :]
    targets = jnp.arange(step_count, dtype=jnp.int32)
    row_rank = step_count + jnp.sum(jnp.where(matches, targets[None, :] - step_count, 0), axis=1)
    selector = (
        (block_columns[:, :, None] == targets[None, None, :])
        & (targets[None, None, :] < row_rank[:, None, None])
    ).astype(jnp.float32)
    current = right_sides
    solved = []
    for column in range(step_count):
        owner_index = pivot_rows[column] // row_count
        slot_index = pivot_rows[column] % row_count
        pivot_side = lax.dynamic_index_in_dim(current, slot_index, 0, keepdims=False)
        candidate = jnp.dot(diag_inverse[column], pivot_side, precision=highest)
        solved_now = spread(candidate, "rows", owner_index)
        column_part = jnp.einsum(
            "rs,rsab->rab", selector[:, :, column], factor_blocks, precision=highest
        )

        def apply_block(piece, start, solved_now=solved_now):
            return jnp.einsum("rab,bn->ran", piece, solved_now, precision=highest)

        correction = apply_block(
            lax.all_gather(column_part, "samp", axis=1, tiled=True), jnp.int32(0)
        )
        current = current - correction
        solved.append(solved_now)
    return (jnp.stack(solved), current)


def solution(mesh):
    placed = (P("rows", None, "samp"), P("rows", None, "samp", None), P("rows", None), P(), P())
    return jax.shard_map(
        local,
        mesh=mesh,
        in_specs=placed,
        out_specs=(P(None, None, "samp"), P("rows", None, "samp")),
        check_vma=False,
    )
```

profile of v0, /device:TPU:1, one launch (start us, length us, event | category | flops | bytes accessed | tf_op | source)
XLA Modules:
  0.0 864.1 jit_solution(17479028503229165503)
XLA Ops:
  11.7 1.8 fusion.23
  20.5 97.0 %all-reduce.9.cloned.1.call-done = f32[128,128]{0,1:T(8,128)} async-done(((f32[128,128]{0,1:T(8,128)}), f32[128,128]{0,1:T(8,128)}) %all-reduce.9.cloned.1.call-update) | async-done | bytes 65552 | tf_op jit(solution)/shard_map/psum | solution.py:9
  117.5 3.9 convolution_subtract_fusion.7
  128.8 93.2 %all-reduce.11.cloned.1.call-done = f32[128,128]{0,1:T(8,128)} async-done(((f32[128,128]{0,1:T(8,128)}), f32[128,128]{0,1:T(8,128)}) %all-reduce.11.cloned.1.call-update) | async-done | bytes 65552 | tf_op jit(solution)/shard_map/psum | solution.py:9
  222.0 4.4 convolution_subtract_fusion.6
  226.5 1.8 fusion.21
  231.9 94.0 %all-reduce.13.cloned.1.call-done = f32[128,128]{0,1:T(8,128)} async-done(((f32[128,128]{0,1:T(8,128)}), f32[128,128]{0,1:T(8,128)}) %all-reduce.13.cloned.1.call-update) | async-done | bytes 65552 | tf_op jit(solution)/shard_map/psum | solution.py:9
  325.8 3.9 convolution_subtract_fusion.5
  331.1 1.7 fusion.20
  336.6 94.2 %all-reduce.15.cloned.1.call-done = f32[128,128]{0,1:T(8,128)} async-done(((f32[128,128]{0,1:T(8,128)}), f32[128,128]{0,1:T(8,128)}) %all-reduce.15.cloned.1.call-update) | async-done | bytes 65552 | tf_op jit(solution)/shard_map/psum | solution.py:9
  430.8 4.4 convolution_subtract_fusion.4
  435.2 1.8 fusion.19
  440.8 93.8 %all-reduce.17.cloned.1.call-done = f32[128,128]{0,1:T(8,128)} async-done(((f32[128,128]{0,1:T(8,128)}), f32[128,128]{0,1:T(8,128)}) %all-reduce.17.cloned.1.call-update) | async-done | bytes 65552 | tf_op jit(solution)/shard_map/psum | solution.py:9
  534.6 3.9 convolution_subtract_fusion.3
  539.9 1.7 fusion.18
  545.0 94.6 %all-reduce.19.cloned.1.call-done = f32[128,128]{0,1:T(8,128)} async-done(((f32[128,128]{0,1:T(8,128)}), f32[128,128]{0,1:T(8,128)}) %all-reduce.19.cloned.1.call-update) | async-done | bytes 65552 | tf_op jit(solution)/shard_map/psum | solution.py:9
  639.6 4.4 convolution_subtract_fusion.2
  644.0 1.8 fusion.17
  648.4 95.0 %all-reduce.21.cloned.1.call-done = f32[128,128]{0,1:T(8,128)} async-done(((f32[128,128]{0,1:T(8,128)}), f32[128,128]{0,1:T(8,128)}) %all-reduce.21.cloned.1.call-update) | async-done | bytes 65552 | tf_op jit(solution)/shard_map/psum | solution.py:9
  743.4 3.9 convolution_subtract_fusion.1
  748.7 1.8 fusion.16
  759.0 89.1 %all-reduce.23.cloned.1.call-done = f32[128,128]{0,1:T(8,128)} async-done(((f32[128,128]{0,1:T(8,128)}), f32[128,128]{0,1:T(8,128)}) %all-reduce.23.cloned.1.call-update) | async-done | bytes 65552 | tf_op jit(solution)/shard_map/psum | solution.py:9
  849.5 2.0 copy.34
  851.6 5.1 convolution_subtract_fusion
  (95 shorter events, 33.9 us)
Async XLA Ops:
  8.0 7.2 copy-start
  8.0 109.5 %copy-start.6 = (f32[36,128,128]{2,1,0:T(8,128)S(1)}, f32[36,128,128]{2,1,0:T(8,128)}, u32[]{:S(2)}) copy-start(f32[36,128,128]{2,1,0:T(8,128)} %param.5) | copy-start | bytes 7077892
  8.0 109.5 %all-reduce.9.cloned.1.call-start = ((), (), s32[]{:S(2)}) async-start(), calls=%async_computation | async-start | bytes 131072 | tf_op jit(solution)/shard_map/psum | solution.py:9
  13.5 104.0 %all-gather.9.cloned.1.call-start = ((), (), s32[]{:S(2)}) async-start(), calls=%async_computation.1 | async-start | bytes 2506752 | tf_op jit(solution)/shard_map/all_gather | solution.py:40
  16.7 112.2 %all-gather.11.cloned.1.call-start = ((), (), s32[]{:S(2)}) async-start(), calls=%async_computation.3 | async-start | bytes 2506752 | tf_op jit(solution)/shard_map/all_gather | solution.py:40
  18.4 203.7 %all-reduce.11.cloned.1.call-start = ((), (), s32[]{:S(2)}) async-start(), calls=%async_computation.2 | async-start | bytes 131072 | tf_op jit(solution)/shard_map/psum | solution.py:9
  121.4 1.4 copy-start.2
  124.6 107.3 %all-gather.13.cloned.1.call-start = ((), (), s32[]{:S(2)}) async-start(), calls=%async_computation.5 | async-start | bytes 2506752 | tf_op jit(solution)/shard_map/all_gather | solution.py:40
  126.1 199.7 %all-reduce.13.cloned.1.call-start = ((), (), s32[]{:S(2)}) async-start(), calls=%async_computation.4 | async-start | bytes 131072 | tf_op jit(solution)/shard_map/psum | solution.py:9
  228.2 108.3 %all-gather.15.cloned.1.call-start = ((), (), s32[]{:S(2)}) async-start(), calls=%async_computation.7 | async-start | bytes 2506752 | tf_op jit(solution)/shard_map/all_gather | solution.py:40
  229.8 201.0 %all-reduce.15.cloned.1.call-start = ((), (), s32[]{:S(2)}) async-start(), calls=%async_computation.6 | async-start | bytes 131072 | tf_op jit(solution)/shard_map/psum | solution.py:9
  332.9 107.9 %all-gather.17.cloned.1.call-start = ((), (), s32[]{:S(2)}) async-start(), calls=%async_computation.9 | async-start | bytes 2506752 | tf_op jit(solution)/shard_map/all_gather | solution.py:40
  334.6 200.0 %all-reduce.17.cloned.1.call-start = ((), (), s32[]{:S(2)}) async-start(), calls=%async_computation.8 | async-start | bytes 131072 | tf_op jit(solution)/shard_map/psum | solution.py:9
  437.0 108.0 %all-gather.19.cloned.1.call-start = ((), (), s32[]{:S(2)}) async-start(), calls=%async_computation.11 | async-start | bytes 2506752 | tf_op jit(solution)/shard_map/all_gather | solution.py:40
  438.5 201.1 %all-reduce.19.cloned.1.call-start = ((), (), s32[]{:S(2)}) async-start(), calls=%async_computation.10 | async-start | bytes 131072 | tf_op jit(solution)/shard_map/psum | solution.py:9
  541.7 106.7 %all-gather.21.cloned.1.call-start = ((), (), s32[]{:S(2)}) async-start(), calls=%async_computation.13 | async-start | bytes 2506752 | tf_op jit(solution)/shard_map/all_gather | solution.py:40
  543.2 200.2 %all-reduce.21.cloned.1.call-start = ((), (), s32[]{:S(2)}) async-start(), calls=%async_computation.12 | async-start | bytes 131072 | tf_op jit(solution)/shard_map/psum | solution.py:9
  645.8 202.2 %all-reduce.23.cloned.1.call-start = ((), (), s32[]{:S(2)}) async-start(), calls=%async_computation.14 | async-start | bytes 131072 | tf_op jit(solution)/shard_map/psum | solution.py:9
  648.3 103.7 %copy-start.7 = (f32[128,128]{0,1:T(8,128)S(1)}, f32[128,128]{0,1:T(8,128)}, u32[]{:S(2)}) copy-start(f32[128,128]{0,1:T(8,128)} %all-reduce.9.cloned.1.call-done) | copy-start | bytes 196612
  648.3 104.3 %copy-start.8 = (f32[128,128]{0,1:T(8,128)S(1)}, f32[128,128]{0,1:T(8,128)}, u32[]{:S(2)}) copy-start(f32[128,128]{0,1:T(8,128)} %all-reduce.11.cloned.1.call-done) | copy-start | bytes 196612
  648.3 105.0 %copy-start.9 = (f32[128,128]{0,1:T(8,128)S(1)}, f32[128,128]{0,1:T(8,128)}, u32[]{:S(2)}) copy-start(f32[128,128]{0,1:T(8,128)} %all-reduce.13.cloned.1.call-done) | copy-start | bytes 196612
  648.4 105.6 %copy-start.10 = (f32[128,128]{0,1:T(8,128)S(1)}, f32[128,128]{0,1:T(8,128)}, u32[]{:S(2)}) copy-start(f32[128,128]{0,1:T(8,128)} %all-reduce.15.cloned.1.call-done) | copy-start | bytes 196612
  750.4 101.1 %copy-start.5 = (f32[36,128,128]{2,1,0:T(8,128)S(1)}, f32[36,128,128]{2,1,0:T(8,128)}, u32[]{:S(2)}) copy-start(f32[36,128,128]{2,1,0:T(8,128)} %copy-done.4) | copy-start | bytes 7077892
  750.5 101.1 %all-gather.23.cloned.1.call-start = ((), (), s32[]{:S(2)}) async-start(), calls=%async_computation.15 | async-start | bytes 2506752 | tf_op jit(solution)/shard_map/all_gather | solution.py:40
  (3 other events, 4.2 us)
Sparse Core Ops, SparseCore 0:
  13.6 103.8 all-reduce.8
  124.7 97.2 all-reduce.10
  228.4 97.4 all-reduce.12
  333.0 97.7 all-reduce.14
  437.1 97.4 all-reduce.16
  541.8 97.7 all-reduce.18
  645.9 97.4 all-reduce.20
  750.6 97.4 all-reduce.22
Sparse Core Ops, SparseCore 1:
  17.2 56.2 all-gather.8
  75.8 53.0 all-gather.10
  132.0 52.8 all-gather.12
  231.4 50.5 all-gather.14
  337.0 50.5 all-gather.16
  440.2 50.5 all-gather.18
  545.4 50.5 all-gather.20
  753.4 50.5 all-gather.22
where the time goes:
time: 865 us; the launch traced here: 864 us
  waiting for transfers between devices  752 us (87%)
  matrix products  59.6 us (7%)
  between operations  31.1 us (4%)
  local copies, waits for them, and re-layouts  18.8 us (2%)
    psum x8, waiting for transfers between devices, spread(): return lax.psum(block, axis)  751 us
    dot_general x8, matrix products, apply_block(): return jnp.einsum('rab,bn->ran', piece, solved_now, precision=highest)  33.8 us
  transfers between devices with their start and end apart: 16, of which 9 were waited for; matrix products, arithmetic and copies ran while one was open for 7% of the time, Pallas kernels for 0%

commit v1 on v0

--- a/solution.py
+++ b/solution.py
@@ -6,7 +6,12 @@
 
 def spread(block, axis, source):
     block = jnp.where(lax.axis_index(axis) == source, block, jnp.zeros_like(block))
-    return lax.psum(block, axis)
+
+    def _advance_column(local_block):
+        r_now = lax.all_gather(local_block, axis)
+        return jnp.sum(r_now, 0)
+
+    return _advance_column(block)
 
 
 def local(right_sides, factor_blocks, block_columns, pivot_rows, diag_inverse):

time: 865 us -> 821 us (0.949)
  waiting for transfers between devices: 752 us -> 695 us
  local copies, waits for them, and re-layouts: 18.8 us -> 30.7 us
    psum x8 -> x0, waiting for transfers between devices: 751 us -> none  [spread(): return lax.psum(block, axis)]
    all_gather x8, waiting for transfers between devices: 0.96 us -> 419 us  [local(): lax.all_gather(column_part, 'samp', axis=1, tiled=True)]
    all_gather x0 -> x8, waiting for transfers between devices: none -> 275 us  [_advance_column(): r_now = lax.all_gather(local_block, axis)]
    unnamed x30 -> x36, local copies, waits for them, and re-layouts: 14.6 us -> 27.4 us
  transfers between devices with their start and end apart: 16 -> 16, of which waited for: 9 -> 16; matrix products, arithmetic and copies ran while one was open for 7% -> 5% of each run, Pallas kernels for 0% -> 0%
where the time goes in v1:
time: 821 us; the launch traced here: 820 us
  waiting for transfers between devices  695 us (85%)
  matrix products  59 us (7%)
  local copies, waits for them, and re-layouts  30.7 us (4%)
  between operations  29.7 us (4%)
    all_gather x8, waiting for transfers between devices, local(): lax.all_gather(column_part, 'samp', axis=1, tiled=True)  419 us
    all_gather x8, waiting for transfers between devices, _advance_column(): r_now = lax.all_gather(local_block, axis)  275 us
    dot_general x8, matrix products, apply_block(): return jnp.einsum('rab,bn->ran', piece, solved_now, precision=highest)  33.2 us
    unnamed x36, local copies, waits for them, and re-layouts  27.4 us
  transfers between devices with their start and end apart: 16, of which 16 were waited for; matrix products, arithmetic and copies ran while one was open for 5% of the time, Pallas kernels for 0%

profile of v1, /device:TPU:1, one launch (start us, length us, event | category | flops | bytes accessed | tf_op | source)
XLA Modules:
  0.0 819.5 jit_solution(9201285238681898394)
XLA Ops:
  17.8 36.8 %all-gather.41.cloned.1.call-done = f32[2048,128]{0,1:T(8,128)} async-done(((f32[128,128]{0,1:T(8,128)}), f32[2048,128]{0,1:T(8,128)}) %all-gather.41.cloned.1.call-update) | async-done | bytes 1048592 | tf_op jit(solution)/shard_map/all_gather | solution.py:11
  56.2 53.1 %all-gather.25.cloned.1.call-done = f32[36,128,128]{2,1,0:T(8,128)} async-done(((f32[36,8,128]{2,1,0:T(8,128)}), f32[36,128,128]{2,1,0:T(8,128)}) %all-gather.25.cloned.1.call-update) | async-done | bytes 2359312 | tf_op jit(solution)/shard_map/all_gather | solution.py:45
  109.3 3.9 convolution_subtract_fusion.7
  120.2 34.7 %all-gather.43.cloned.1.call-done = f32[2048,128]{0,1:T(8,128)} async-done(((f32[128,128]{0,1:T(8,128)}), f32[2048,128]{0,1:T(8,128)}) %all-gather.43.cloned.1.call-update) | async-done | bytes 1048592 | tf_op jit(solution)/shard_map/all_gather | solution.py:11
  156.5 53.0 %all-gather.27.cloned.1.call-done = f32[36,128,128]{2,1,0:T(8,128)} async-done(((f32[36,8,128]{2,1,0:T(8,128)}), f32[36,128,128]{2,1,0:T(8,128)}) %all-gather.27.cloned.1.call-update) | async-done | bytes 2359312 | tf_op jit(solution)/shard_map/all_gather | solution.py:45
  209.4 4.4 convolution_subtract_fusion.6
  219.0 35.1 %all-gather.45.cloned.1.call-done = f32[2048,128]{0,1:T(8,128)} async-done(((f32[128,128]{0,1:T(8,128)}), f32[2048,128]{0,1:T(8,128)}) %all-gather.45.cloned.1.call-update) | async-done | bytes 1048592 | tf_op jit(solution)/shard_map/all_gather | solution.py:11
  255.7 53.0 %all-gather.29.cloned.1.call-done = f32[36,128,128]{2,1,0:T(8,128)} async-done(((f32[36,8,128]{2,1,0:T(8,128)}), f32[36,128,128]{2,1,0:T(8,128)}) %all-gather.29.cloned.1.call-update) | async-done | bytes 2359312 | tf_op jit(solution)/shard_map/all_gather | solution.py:45
  308.7 3.9 convolution_subtract_fusion.5
  319.6 34.7 %all-gather.47.cloned.1.call-done = f32[2048,128]{0,1:T(8,128)} async-done(((f32[128,128]{0,1:T(8,128)}), f32[2048,128]{0,1:T(8,128)}) %all-gather.47.cloned.1.call-update) | async-done | bytes 1048592 | tf_op jit(solution)/shard_map/all_gather | solution.py:11
  355.8 53.1 %all-gather.31.cloned.1.call-done = f32[36,128,128]{2,1,0:T(8,128)} async-done(((f32[36,8,128]{2,1,0:T(8,128)}), f32[36,128,128]{2,1,0:T(8,128)}) %all-gather.31.cloned.1.call-update) | async-done | bytes 2359312 | tf_op jit(solution)/shard_map/all_gather | solution.py:45
  408.9 3.9 convolution_subtract_fusion.4
  419.6 34.9 %all-gather.49.cloned.1.call-done = f32[2048,128]{0,1:T(8,128)} async-done(((f32[128,128]{0,1:T(8,128)}), f32[2048,128]{0,1:T(8,128)}) %all-gather.49.cloned.1.call-update) | async-done | bytes 1048592 | tf_op jit(solution)/shard_map/all_gather | solution.py:11
  456.7 52.3 %all-gather.33.cloned.1.call-done = f32[36,128,128]{2,1,0:T(8,128)} async-done(((f32[36,8,128]{2,1,0:T(8,128)}), f32[36,128,128]{2,1,0:T(8,128)}) %all-gather.33.cloned.1.call-update) | async-done | bytes 2359312 | tf_op jit(solution)/shard_map/all_gather | solution.py:45
  509.0 3.9 convolution_subtract_fusion.3
  519.7 34.9 %all-gather.51.cloned.1.call-done = f32[2048,128]{0,1:T(8,128)} async-done(((f32[128,128]{0,1:T(8,128)}), f32[2048,128]{0,1:T(8,128)}) %all-gather.51.cloned.1.call-update) | async-done | bytes 1048592 | tf_op jit(solution)/shard_map/all_gather | solution.py:11
  556.8 52.3 %all-gather.35.cloned.1.call-done = f32[36,128,128]{2,1,0:T(8,128)} async-done(((f32[36,8,128]{2,1,0:T(8,128)}), f32[36,128,128]{2,1,0:T(8,128)}) %all-gather.35.cloned.1.call-update) | async-done | bytes 2359312 | tf_op jit(solution)/shard_map/all_gather | solution.py:45
  609.1 4.4 convolution_subtract_fusion.2
  619.3 34.5 %all-gather.53.cloned.1.call-done = f32[2048,128]{0,1:T(8,128)} async-done(((f32[128,128]{0,1:T(8,128)}), f32[2048,128]{0,1:T(8,128)}) %all-gather.53.cloned.1.call-update) | async-done | bytes 1048592 | tf_op jit(solution)/shard_map/all_gather | solution.py:11
  656.0 52.4 %all-gather.37.cloned.1.call-done = f32[36,128,128]{2,1,0:T(8,128)} async-done(((f32[36,8,128]{2,1,0:T(8,128)}), f32[36,128,128]{2,1,0:T(8,128)}) %all-gather.37.cloned.1.call-update) | async-done | bytes 2359312 | tf_op jit(solution)/shard_map/all_gather | solution.py:45
  708.4 3.9 convolution_subtract_fusion.1
  724.2 29.8 %all-gather.55.cloned.1.call-done = f32[2048,128]{0,1:T(8,128)} async-done(((f32[128,128]{0,1:T(8,128)}), f32[2048,128]{0,1:T(8,128)}) %all-gather.55.cloned.1.call-update) | async-done | bytes 1048592 | tf_op jit(solution)/shard_map/all_gather | solution.py:11
  758.2 49.7 %all-gather.39.cloned.1.call-done = f32[36,128,128]{2,1,0:T(8,128)} async-done(((f32[36,8,128]{2,1,0:T(8,128)}), f32[36,128,128]{2,1,0:T(8,128)}) %all-gather.39.cloned.1.call-update) | async-done | bytes 2359312 | tf_op jit(solution)/shard_map/all_gather | solution.py:45
  807.9 5.1 convolution_subtract_fusion
  (109 shorter events, 62.4 us)
Async XLA Ops:
  7.2 7.2 copy-start
  7.2 47.5 %all-gather.41.cloned.1.call-start = ((), (), s32[]{:S(2)}) async-start(), calls=%async_computation.8 | async-start | bytes 1114112 | tf_op jit(solution)/shard_map/all_gather | solution.py:11
  12.6 96.7 %all-gather.25.cloned.1.call-start = ((), (), s32[]{:S(2)}) async-start(), calls=%async_computation | async-start | bytes 2506752 | tf_op jit(solution)/shard_map/all_gather | solution.py:45
  14.3 95.0 %copy-start.9 = (f32[36,128,128]{2,1,0:T(8,128)S(1)}, f32[36,128,128]{2,1,0:T(8,128)}, u32[]{:S(2)}) copy-start(f32[36,128,128]{2,1,0:T(8,128)} %param.5) | copy-start | bytes 7077892
  15.8 139.1 %all-gather.43.cloned.1.call-start = ((), (), s32[]{:S(2)}) async-start(), calls=%async_computation.9 | async-start | bytes 1114112 | tf_op jit(solution)/shard_map/all_gather | solution.py:11
  113.2 1.4 copy-start.6
  116.4 93.1 %all-gather.27.cloned.1.call-start = ((), (), s32[]{:S(2)}) async-start(), calls=%async_computation.1 | async-start | bytes 2506752 | tf_op jit(solution)/shard_map/all_gather | solution.py:45
  118.1 136.1 %all-gather.45.cloned.1.call-start = ((), (), s32[]{:S(2)}) async-start(), calls=%async_computation.10 | async-start | bytes 1114112 | tf_op jit(solution)/shard_map/all_gather | solution.py:11
  215.6 93.1 %all-gather.29.cloned.1.call-start = ((), (), s32[]{:S(2)}) async-start(), calls=%async_computation.2 | async-start | bytes 2506752 | tf_op jit(solution)/shard_map/all_gather | solution.py:45
  217.3 136.9 %all-gather.47.cloned.1.call-start = ((), (), s32[]{:S(2)}) async-start(), calls=%async_computation.11 | async-start | bytes 1114112 | tf_op jit(solution)/shard_map/all_gather | solution.py:11
  312.5 1.4 copy-start.1
  315.7 93.2 %all-gather.31.cloned.1.call-start = ((), (), s32[]{:S(2)}) async-start(), calls=%async_computation.3 | async-start | bytes 2506752 | tf_op jit(solution)/shard_map/all_gather | solution.py:45
  316.1 92.8 %copy-start.2 = (f32[36,128,128]{2,1,0:T(8,128)S(1)}, f32[36,128,128]{2,1,0:T(8,128)}, u32[]{:S(2)}) copy-start(f32[36,128,128]{2,1,0:T(8,128)} %copy-done.1) | copy-start | bytes 7077892
  317.6 136.9 %all-gather.49.cloned.1.call-start = ((), (), s32[]{:S(2)}) async-start(), calls=%async_computation.12 | async-start | bytes 1114112 | tf_op jit(solution)/shard_map/all_gather | solution.py:11
  412.8 1.4 copy-start.3
  416.0 93.0 %all-gather.33.cloned.1.call-start = ((), (), s32[]{:S(2)}) async-start(), calls=%async_computation.4 | async-start | bytes 2506752 | tf_op jit(solution)/shard_map/all_gather | solution.py:45
  416.1 92.9 %copy-start.4 = (f32[36,128,128]{2,1,0:T(8,128)S(1)}, f32[36,128,128]{2,1,0:T(8,128)}, u32[]{:S(2)}) copy-start(f32[36,128,128]{2,1,0:T(8,128)} %copy-done.3) | copy-start | bytes 7077892
  417.6 136.9 %all-gather.51.cloned.1.call-start = ((), (), s32[]{:S(2)}) async-start(), calls=%async_computation.13 | async-start | bytes 1114112 | tf_op jit(solution)/shard_map/all_gather | solution.py:11
  516.1 93.1 %all-gather.35.cloned.1.call-start = ((), (), s32[]{:S(2)}) async-start(), calls=%async_computation.5 | async-start | bytes 2506752 | tf_op jit(solution)/shard_map/all_gather | solution.py:45
  517.7 136.1 %all-gather.53.cloned.1.call-start = ((), (), s32[]{:S(2)}) async-start(), calls=%async_computation.14 | async-start | bytes 1114112 | tf_op jit(solution)/shard_map/all_gather | solution.py:11
  615.3 93.1 %all-gather.37.cloned.1.call-start = ((), (), s32[]{:S(2)}) async-start(), calls=%async_computation.6 | async-start | bytes 2506752 | tf_op jit(solution)/shard_map/all_gather | solution.py:45
  617.2 136.7 %all-gather.55.cloned.1.call-start = ((), (), s32[]{:S(2)}) async-start(), calls=%async_computation.15 | async-start | bytes 1114112 | tf_op jit(solution)/shard_map/all_gather | solution.py:11
  715.4 92.5 %all-gather.39.cloned.1.call-start = ((), (), s32[]{:S(2)}) async-start(), calls=%async_computation.7 | async-start | bytes 2506752 | tf_op jit(solution)/shard_map/all_gather | solution.py:45
  721.1 86.8 %copy-start.8 = (f32[36,128,128]{2,1,0:T(8,128)S(1)}, f32[36,128,128]{2,1,0:T(8,128)}, u32[]{:S(2)}) copy-start(f32[36,128,128]{2,1,0:T(8,128)} %copy-done.7) | copy-start | bytes 7077892
  (2 other events, 2.8 us)
Sparse Core Ops, SparseCore 0:
  12.8 41.8 all-gather.40
  57.6 51.6 all-gather.24
  116.5 38.3 all-gather.42
  157.7 51.6 all-gather.26
  215.7 38.3 all-gather.44
  257.0 51.6 all-gather.28
  315.8 38.3 all-gather.46
  357.2 51.6 all-gather.30
  416.1 38.3 all-gather.48
  457.3 51.6 all-gather.32
  516.2 38.3 all-gather.50
  557.4 51.6 all-gather.34
  615.4 38.3 all-gather.52
  656.7 51.6 all-gather.36
  715.6 38.3 all-gather.54
  756.2 51.6 all-gather.38
